TPU v7x, 32 devices: a whole 2x2x4 slice. The times are simulated.
32 devices in a mesh: dp: 2 (over core), seq: 8 (over z, x), mp: 2 (over y).
Axes of the slice: x: 2, y: 2, z: 4, core: 2. Of those that a mesh axis runs over, the one named last changes fastest.
Arguments:
- queries: bfloat16 [6, 1024, 4096], P('dp', 'seq', 'mp'), may hold values from -1000 to 1000
- database: bfloat16 [256, 128, 1024], P('seq', None, 'mp'), may hold values from -300 to 300
- owner_ids: int32 [2, 8, 6, 2], P('dp'), may hold values from 0 to 7, all different within a row; in each aligned block of 6 rows (0 to 5, 6 to 11, ..., all dimensions but the last counted through in order) at most 2 rows name the same one
- row_ids: int32 [2, 8, 6, 2], P('dp'), may hold values from 0 to 31
- pre_gain: float32 [1024], replicated, may hold values from 0.1 to 1.9
- out_gain: float32 [1024], replicated, may hold values from 0.1 to 1.9
- w_in: bfloat16 [1024, 4096], P(None, 'mp'), may hold values from -0.1875 to 0.1875
- w_out: bfloat16 [4096, 1024], P('mp'), may hold values from -0.09375 to 0.09375
- w_key: bfloat16 [1024, 4096], P(None, 'mp'), may hold values from -0.1875 to 0.1875
- w_value: bfloat16 [1024, 4096], P(None, 'mp'), may hold values from -0.1875 to 0.1875
Outputs:
- attended: bfloat16 [6, 1024, 4096], P('dp', 'seq', 'mp')
Inputs may be any that keep to these rules, and one draw needn't show every extreme that they name: `owner_ids`: within one index pair of the first two dimensions (the 6 spans of one device) no shard number appears more than 2 times, and the 2 neighbours of one span lie on different shards.
All inputs are finite; a program needn't handle non-finite values.
Results may differ from a plain program's by a relative error of at most 0.04.
Values may be sent and summed in bfloat16 or wider, within the bound.
A program may use at most 64 MiB of HBM per device.

v0:
```python
import functools

import jax
import jax.numpy as jnp
from jax import lax
from jax.experimental import pallas as pl
from jax.experimental.pallas import tpu as pltpu
from jax.sharding import PartitionSpec as P


HD = 128
MOST = 2
CHUNKS = 2

epsilon = 1e-06


def rms_scale(values, gain_values):
    return (
        values
        * lax.rsqrt(jnp.mean(values * values, axis=-1, keepdims=True) + epsilon)
        * gain_values
    )


def send_kernel(shards, requests, my_ref, owner_ref, row_ref, database_ref, *refs):
    out_refs, (wanted_ref, stage, in_sem, out_sem) = refs[:CHUNKS], refs[CHUNKS:]
    my_index = my_ref[0]
    rows = stage.shape[1] // CHUNKS

    def fetch(slot):
        return pltpu.make_async_copy(
            database_ref.at[wanted_ref[slot]], stage.at[slot], in_sem.at[slot]
        )

    def emit(slot, chunk):
        return pltpu.make_async_copy(
            stage.at[slot, pl.ds(chunk * rows, rows)],
            out_refs[chunk].at[slot],
            out_sem.at[chunk, slot],
        )

    @pl.loop(0, shards)
    def _(peer):
        for rank in range(MOST):
            wanted_ref[peer * MOST + rank] = 0
        rank = jnp.int32(0)
        for i in range(requests):
            mine = owner_ref[peer * requests + i] == my_index

            @pl.when(mine)
            def _():
                wanted_ref[peer * MOST + jnp.minimum(rank, MOST - 1)] = row_ref[
                    peer * requests + i
                ]

            rank = rank + mine.astype(jnp.int32)
        for rank in range(MOST):
            fetch(peer * MOST + rank).start()

    @pl.loop(0, shards * MOST)
    def _(slot):
        fetch(slot).wait()
        for chunk in range(CHUNKS):
            emit(slot, chunk).start()

    @pl.loop(0, shards * MOST)
    def _(slot):
        for chunk in range(CHUNKS):
            emit(slot, chunk).wait()


def gather_requests(database, owners, row_index, my_index, shards, requests):
    slots = shards * MOST
    block_len, width = database.shape[1:]
    piece = jax.ShapeDtypeStruct((slots, block_len // CHUNKS, width), database.dtype)
    return pl.pallas_call(
        functools.partial(send_kernel, shards, requests),
        out_shape=[piece] * CHUNKS,
        in_specs=[pl.BlockSpec(memory_space=pltpu.SMEM)] * 3
        + [pl.BlockSpec(memory_space=pl.ANY)],
        out_specs=[pl.BlockSpec(memory_space=pl.ANY)] * CHUNKS,
        scratch_shapes=[
            pltpu.SMEM((slots,), jnp.int32),
            pltpu.VMEM((slots, block_len, width), database.dtype),
            pltpu.SemaphoreType.DMA((slots,)),
            pltpu.SemaphoreType.DMA((CHUNKS, slots)),
        ],
        name="gather_requests",
    )(my_index, owners, row_index, database)


def pick_kernel(
    shards, requests, per_span, neigh, my_ref, owner_ref, arrived_ref, kept_ref, passed_ref,
    source_ref, count_ref, stage, in_sem, out_sem,
):
    my_index = my_ref[0]

    @pl.loop(0, shards)
    def _(shard):
        count_ref[shard] = 0

    for i in range(requests):
        owner = owner_ref[my_index * requests + i]
        rank = count_ref[owner]
        count_ref[owner] = rank + 1
        source_ref[i] = owner * MOST + jnp.minimum(rank, MOST - 1)

    def fetch(i):
        return pltpu.make_async_copy(
            arrived_ref.at[source_ref[i]], stage.at[i], in_sem.at[i]
        )

    def emit(i):
        sequence, span, place = (
            i // (per_span * neigh), (i // neigh) % per_span, i % neigh,
        )
        if span == per_span - 1:
            target = passed_ref.at[sequence * neigh + place]
        else:
            target = kept_ref.at[(sequence * (per_span - 1) + span) * neigh + place]
        return pltpu.make_async_copy(stage.at[i], target, out_sem.at[i])

    for i in range(requests):
        fetch(i).start()
    for i in range(requests):
        fetch(i).wait()
        emit(i).start()
    for i in range(requests):
        emit(i).wait()


def pick_blocks(arrived, owners, my_index, shards, requests, per_span, neigh):
    _, rows, width = arrived.shape
    sequences = requests // (per_span * neigh)
    passed_count = sequences * neigh
    return pl.pallas_call(
        functools.partial(pick_kernel, shards, requests, per_span, neigh),
        out_shape=[
            jax.ShapeDtypeStruct((requests - passed_count, rows, width), arrived.dtype),
            jax.ShapeDtypeStruct((passed_count, rows, width), arrived.dtype),
        ],
        in_specs=[pl.BlockSpec(memory_space=pltpu.SMEM)] * 2
        + [pl.BlockSpec(memory_space=pl.ANY)],
        out_specs=[pl.BlockSpec(memory_space=pl.ANY)] * 2,
        scratch_shapes=[
            pltpu.SMEM((requests,), jnp.int32),
            pltpu.SMEM((shards,), jnp.int32),
            pltpu.VMEM((requests, rows, width), arrived.dtype),
            pltpu.SemaphoreType.DMA((requests,)),
            pltpu.SemaphoreType.DMA((requests,)),
        ],
        name="pick_blocks",
    )(my_index, owners, arrived)


def attend_kernel(has_ref, query_ref, *refs):
    key_refs, value_refs = refs[:CHUNKS], refs[CHUNKS : 2 * CHUNKS]
    out_ref = refs[-1]
    keep = has_ref[0] > 0
    local_width = query_ref.shape[-1]
    heads = local_width // HD
    group = 4 if heads % 4 == 0 else 1
    span_len = query_ref.shape[1]

    def merged(part_refs, columns):
        pieces = []
        for ref in part_refs:
            piece = ref[0, :, :, columns]
            pieces.append(piece.reshape(-1, HD))
        return jnp.concatenate(pieces, axis=0)

    for first in range(0, heads, group):
        spots = [slice((first + i) * HD, (first + i + 1) * HD) for i in range(group)]
        scores = jnp.concatenate(
            [
                lax.dot_general(
                    query_ref[0, :, spot],
                    merged(key_refs, spot),
                    (((1,), (1,)), ((), ())),
                    preferred_element_type=jnp.float32,
                )
                for spot in spots
            ],
            axis=0,
        )
        scores = scores * HD ** (-0.5)
        weights = jnp.exp(scores - jnp.max(scores, axis=-1, keepdims=True))
        inverse = 1.0 / jnp.sum(weights, axis=-1, keepdims=True)
        weights = weights.astype(jnp.bfloat16)
        for i, spot in enumerate(spots):
            rows = slice(i * span_len, (i + 1) * span_len)
            attended = jnp.dot(
                weights[rows], merged(value_refs, spot), preferred_element_type=jnp.float32
            )
            out_ref[0, :, spot] = jnp.where(keep, attended * inverse[rows], 0.0).astype(
                out_ref.dtype
            )


def attend(span, per_span, has_source, queries, keys, values, out, group, offset):
    sequences, length, local_width = queries.shape
    span_len = length // per_span
    _, neigh, rows, _ = keys[0].shape
    query_spec = pl.BlockSpec((1, span_len, local_width), lambda q: (q, span, 0))
    block_spec = pl.BlockSpec(
        (1, neigh, rows, local_width), lambda q: (q * group + offset, 0, 0, 0)
    )
    fresh = out is None
    operands = [has_source, queries, *keys, *values, queries if fresh else out]
    keys_total = neigh * rows * CHUNKS * sequences
    return pl.pallas_call(
        attend_kernel,
        grid=(sequences,),
        out_shape=jax.ShapeDtypeStruct(queries.shape, queries.dtype),
        in_specs=[pl.BlockSpec(memory_space=pltpu.SMEM), query_spec]
        + [block_spec] * (2 * CHUNKS)
        + [pl.BlockSpec(memory_space=pl.ANY)],
        out_specs=query_spec,
        input_output_aliases={} if fresh else {len(operands) - 1: 0},
        cost_estimate=pl.CostEstimate(
            flops=4 * keys_total * span_len * local_width,
            bytes_accessed=4 * keys_total * local_width,
            transcendentals=keys_total * span_len * (local_width // HD),
        ),
        name="attend",
    )(*operands)


def join_kernel(me_ref, gain_ref, *refs):
    held_refs, (full_ref, normed_ref) = refs[:-2], refs[-2:]
    peers, width = len(held_refs), held_refs[0].shape[-1]
    pieces = [ref[...].astype(jnp.float32) for ref in held_refs]
    squares = sum(jnp.sum(piece * piece, axis=-1, keepdims=True) for piece in pieces)
    scale = lax.rsqrt(squares / (width * peers) + epsilon)
    for by in range(peers):
        owner = lax.rem(me_ref[0] - by + peers, peers)
        columns = pl.ds(pl.multiple_of(owner * width, width), width)
        full_ref[:, columns] = held_refs[by][...]
        normed_ref[:, columns] = (pieces[by] * scale * gain_ref[:, columns]).astype(
            normed_ref.dtype
        )


def joined(held, gain, tile):
    peers = len(held)
    me = lax.axis_index("mp").astype(jnp.int32).reshape(1)
    rows, width = held[0].shape
    full = jax.ShapeDtypeStruct((rows, width * peers), held[0].dtype)
    full_spec = pl.BlockSpec((tile, width * peers), lambda i: (i, 0))
    return pl.pallas_call(
        join_kernel,
        grid=(rows // tile,),
        out_shape=[full, full],
        in_specs=[
            pl.BlockSpec(memory_space=pltpu.SMEM),
            pl.BlockSpec((1, width * peers), lambda i: (0, 0)),
        ]
        + [pl.BlockSpec((tile, width), lambda i: (i, 0))] * peers,
        out_specs=[full_spec, full_spec],
        cost_estimate=pl.CostEstimate(
            flops=6 * rows * width * peers, bytes_accessed=6 * rows * width * peers,
            transcendentals=rows,
        ),
        name="joined",
    )(me, gain.reshape(1, -1), *held)


def norm_kernel(gain_ref, *refs):
    total = refs[0][...].astype(jnp.float32)
    for ref in refs[1:-1]:
        total = total + ref[...].astype(jnp.float32)
    refs[-1][...] = rms_scale(total, gain_ref[...]).astype(refs[-1].dtype)


def encoded_rows(terms, gain, tile):
    rows, width = terms[0].shape
    spec = pl.BlockSpec((tile, width), lambda i: (i, 0))
    return pl.pallas_call(
        norm_kernel,
        grid=(rows // tile,),
        out_shape=jax.ShapeDtypeStruct((rows, width), jnp.bfloat16),
        in_specs=[pl.BlockSpec((1, width), lambda i: (0, 0))] + [spec] * len(terms),
        out_specs=spec,
        cost_estimate=pl.CostEstimate(
            flops=6 * rows * width, bytes_accessed=2 * rows * width * (len(terms) + 1),
            transcendentals=rows,
        ),
        name="encoded_rows",
    )(gain.reshape(1, -1), *terms)


def swapped(array, axis, by):
    peers = lax.axis_size(axis)
    return lax.ppermute(array, axis, [(i, (i + by) % peers) for i in range(peers)])


def passed_along(array, axis, by):
    peers = lax.axis_size(axis)
    pairs = [(i, i + by) for i in range(peers) if 0 <= i + by < peers]
    return lax.ppermute(array, axis, pairs)


def step(queries, database, owner_ids, row_ids, pre_gain, out_gain, w_in, w_out, w_key, w_value):
    shards = lax.axis_size("seq")
    my_index = lax.axis_index("seq")
    peers = lax.axis_size("mp")
    sequences, _, local_width = queries.shape
    slot_count, neigh = owner_ids.shape[2:]
    per_span = slot_count // sequences
    requests = slot_count * neigh
    owners = owner_ids.reshape(-1)
    row_index = row_ids.reshape(-1)
    mine = my_index.astype(jnp.int32).reshape(1)
    sending = gather_requests(database, owners, row_index, mine, shards, requests)
    kept, passed = [], []
    for chunk in range(CHUNKS):
        piece = sending[chunk]
        arrived = lax.all_to_all(
            piece.reshape((shards, MOST) + piece.shape[1:]),
            "seq",
            split_axis=0,
            concat_axis=0,
            tiled=True,
        ).reshape(piece.shape)
        stay, leave = pick_blocks(arrived, owners, mine, shards, requests, per_span, neigh)
        kept.append(stay)
        passed.append(passed_along(leave, "seq", 1))

    def encode(own):
        rows = own.shape[1]
        own = own.reshape(-1, own.shape[-1])
        held = [own] + [swapped(own, "mp", by) for by in range(1, peers)]
        blocks, normed = joined(held, pre_gain, neigh * rows)
        hidden = jax.nn.gelu(
            jnp.dot(normed, w_in, preferred_element_type=jnp.float32)
        ).astype(jnp.bfloat16)
        partial = jnp.dot(hidden, w_out, preferred_element_type=jnp.float32).astype(
            jnp.bfloat16
        )
        others = [swapped(partial, "mp", by) for by in range(1, peers)]
        encoded = encoded_rows(
            [blocks, partial, *others], out_gain, neigh * rows
        )
        shape = (-1, neigh, rows, local_width)
        keys = jnp.dot(encoded, w_key, preferred_element_type=jnp.float32).astype(jnp.bfloat16)
        values = jnp.dot(encoded, w_value, preferred_element_type=jnp.float32).astype(
            jnp.bfloat16
        )
        return keys.reshape(shape), values.reshape(shape)

    kept_rows = [encode(piece) for piece in kept]
    passed_rows = [encode(piece) for piece in passed]
    always = jnp.ones((1,), jnp.int32)
    out = None
    for span in range(1, per_span):
        out = attend(
            span, per_span, always, queries, [k for k, _ in kept_rows],
            [v for _, v in kept_rows], out, per_span - 1, span - 1,
        )
    has_source = (my_index > 0).astype(jnp.int32).reshape(1)
    return attend(
        0, per_span, has_source, queries, [k for k, _ in passed_rows],
        [v for _, v in passed_rows], out, 1, 0,
    )


def solution(mesh):
    return jax.shard_map(
        step,
        mesh=mesh,
        in_specs=(
            P("dp", "seq", "mp"),
            P("seq", None, "mp"),
            P("dp", None, None, None),
            P("dp", None, None, None),
            P(),
            P(),
            P(None, "mp"),
            P("mp", None),
            P(None, "mp"),
            P(None, "mp"),
        ),
        out_specs=P("dp", "seq", "mp"),
        check_vma=False,
    )
```

profile of v0, /device:TPU:0, one launch (start us, length us, event | category | flops | bytes accessed | tf_op | source)
XLA Modules:
  0.0 220.6 jit_solution(3454723327851452374)
XLA Ops:
  0.0 0.8 copy.14
  0.8 0.7 reshape.86.owner_ref
  1.5 0.8 copy.15
  2.3 0.7 reshape.87.row_ref
  3.0 3.5 %gather_requests.1 = (bf16[16,64,512]{2,1,0:T(8,128)(2,1)}, bf16[16,64,512]{2,1,0:T(8,128)(2,1)}) custom-call(s32[1]{0:T(128)} %bitcast.4.my_ref, s32[96]{0:T(128)} %reshape.86.owner_ref, s32[96]{0:T(128)} %reshape.87.row_ref, bf16[32,128,512]{2,1,0:T(8,128)(2,1)} %database_ref.1), custom_call_target="tpu_custom_call" | custom-call | tf_op jit(solution)/shard_map/gather_requests/pallas_call | solution.py:77
  6.5 33.2 %all_to_all.10 = bf16[8,2,64,512]{3,2,1,0:T(8,128)(2,1)} all-to-all(bf16[8,2,64,512]{3,2,1,0:T(8,128)(2,1)} %bitcast.60), channel_id=1, replica_groups=mesh['dp'=2,'seq'=8,'mp'=2] {'seq'}, dimensions={0} | all-to-all | bytes 2097152 | tf_op jit(solution)/shard_map/all_to_all | solution.py:319
  39.6 3.6 %all-to-all-start = ((bf16[8,2,64,512]{3,2,1,0:T(8,128)(2,1)}), bf16[8,2,64,512]{3,2,1,0:T(8,128)(2,1)S(1)}, u32[]{:S(2)}, u32[]{:S(2)}) async-start(bf16[8,2,64,512]{3,2,1,0:T(8,128)(2,1)} %bitcast.59), calls=%async_computation | async-start | bytes 2097152 | tf_op jit(solution)/shard_map/all_to_all | solution.py:319
  43.2 2.7 %pick_blocks.3 = (bf16[6,64,512]{2,1,0:T(8,128)(2,1)}, bf16[6,64,512]{2,1,0:T(8,128)(2,1)}) custom-call(s32[1]{0:T(128)} %bitcast.4.my_ref, s32[96]{0:T(128)} %reshape.86.owner_ref, bf16[16,64,512]{2,1,0:T(8,128)(2,1)} %bitcast.50), custom_call_target="tpu_custom_call" | custom-call | tf_op jit(solution)/shard_map/pick_blocks/pallas_call | solution.py:137
  46.0 1.6 collective-permute-start.8
  47.5 21.2 %all-to-all-done = bf16[8,2,64,512]{3,2,1,0:T(8,128)(2,1)S(1)} async-done(((bf16[8,2,64,512]{3,2,1,0:T(8,128)(2,1)}), bf16[8,2,64,512]{3,2,1,0:T(8,128)(2,1)S(1)}, u32[]{:S(2)}, u32[]{:S(2)}) %all-to-all-start) | async-done | bytes 1048608 | tf_op jit(solution)/shard_map/all_to_all | solution.py:319
  68.8 1.0 copy-done
  69.7 2.7 %pick_blocks.2 = (bf16[6,64,512]{2,1,0:T(8,128)(2,1)}, bf16[6,64,512]{2,1,0:T(8,128)(2,1)}) custom-call(s32[1]{0:T(128)} %bitcast.4.my_ref, s32[96]{0:T(128)} %reshape.86.owner_ref, bf16[16,64,512]{2,1,0:T(8,128)(2,1)} %bitcast.49), custom_call_target="tpu_custom_call" | custom-call | tf_op jit(solution)/shard_map/pick_blocks/pallas_call | solution.py:137
  72.5 1.6 collective-permute-start.6
  74.1 3.9 %collective-permute-start.3 = (bf16[6,64,512]{2,1,0:T(8,128)(2,1)}, bf16[6,64,512]{2,1,0:T(8,128)(2,1)}, u32[]{:S(2)}, u32[]{:S(2)}) collective-permute-start(bf16[6,64,512]{2,1,0:T(8,128)(2,1)} %get-tuple-element.24), channel_id=1, source_target_pairs={{0,2},{2,4},{4,6},{6,8},{8,10},{10,12},{12,14},{1,3},{3,5},{5,7},{... | collective-permute-start | bytes 1179656 | tf_op jit(solution)/shard_map/ppermute | solution.py:301
  78.0 1.3 collective-permute-start
  79.3 0.8 copy-done.10
  80.1 3.3 %joined.7 = (bf16[384,1024]{1,0:T(8,128)(2,1)}, bf16[384,1024]{1,0:T(8,128)(2,1)}) custom-call(s32[1]{0:T(128)} %bitcast.2.me_ref, f32[1,1024]{1,0:T(1,128)} %bitcast.67, bf16[384,512]{1,0:T(8,128)(2,1)} %bitcast.64, bf16[384,512]{1,0:T(8,128)(2,1)} %copy-done.10), custom_call_target="tpu_custom_call" | custom-call | flops 2359296 | bytes 2359296 | tf_op jit(solution)/shard_map/joined/pallas_call | solution.py:251
  83.4 7.3 %fusion.65.refs_1_ = bf16[384,1024]{1,0:T(8,128)(2,1)S(1)} fusion(bf16[2048,1024]{1,0:T(8,128)(2,1)} %param.17, bf16[384,1024]{1,0:T(8,128)(2,1)} %get-tuple-element.32, bf16[1024,2048]{1,0:T(8,128)(2,1)} %param.16), kind=kOutput, calls=%fused_computation.67 | convolution fusion | flops 3228696576 | bytes 9961472 | tf_op jit(solution)/shard_map/dot_general | solution.py:338
  90.7 0.6 collective-permute-start.9
  91.2 1.5 collective-permute-start.4
  92.8 0.8 copy-done.11
  93.5 3.3 %joined.6 = (bf16[384,1024]{1,0:T(8,128)(2,1)}, bf16[384,1024]{1,0:T(8,128)(2,1)}) custom-call(s32[1]{0:T(128)} %bitcast.2.me_ref, f32[1,1024]{1,0:T(1,128)} %bitcast.68, bf16[384,512]{1,0:T(8,128)(2,1)} %bitcast.66, bf16[384,512]{1,0:T(8,128)(2,1)} %copy-done.11), custom_call_target="tpu_custom_call" | custom-call | flops 2359296 | bytes 2359296 | tf_op jit(solution)/shard_map/joined/pallas_call | solution.py:251
  96.8 7.3 %fusion.62.refs_1_ = bf16[384,1024]{1,0:T(8,128)(2,1)S(1)} fusion(bf16[2048,1024]{1,0:T(8,128)(2,1)} %param.17, bf16[384,1024]{1,0:T(8,128)(2,1)} %get-tuple-element.29, bf16[1024,2048]{1,0:T(8,128)(2,1)} %param.16), kind=kOutput, calls=%fused_computation.66 | convolution fusion | flops 3228696576 | bytes 9961472 | tf_op jit(solution)/shard_map/dot_general | solution.py:338
  104.1 0.6 collective-permute-start.7
  104.7 1.5 collective-permute-start.1
  106.2 13.5 %collective-permute-done.4.refs_1_ = bf16[384,512]{1,0:T(8,128)(2,1)} collective-permute-done((bf16[384,512]{1,0:T(8,128)(2,1)}, bf16[384,512]{1,0:T(8,128)(2,1)}, u32[]{:S(2)}, u32[]{:S(2)}) %collective-permute-start.4) | collective-permute-done | bytes 393248 | tf_op jit(solution)/shard_map/ppermute | solution.py:295
  119.7 3.3 %joined.5 = (bf16[384,1024]{1,0:T(8,128)(2,1)}, bf16[384,1024]{1,0:T(8,128)(2,1)}) custom-call(s32[1]{0:T(128)} %bitcast.2.me_ref, f32[1,1024]{1,0:T(1,128)} %bitcast.69, bf16[384,512]{1,0:T(8,128)(2,1)} %bitcast.11.refs_0_, bf16[384,512]{1,0:T(8,128)(2,1)} %collective-permute-done.4.refs_1_), custom_call_target="tpu_custom_call" | custom-call | flops 2359296 | bytes 2359296 | tf_op jit(solution)/shard_map/joined/pallas_call | solution.py:251
  122.9 8.2 %fusion.59.refs_1_ = bf16[384,1024]{1,0:T(8,128)(2,1)} fusion(bf16[2048,1024]{1,0:T(8,128)(2,1)} %param.17, bf16[384,1024]{1,0:T(8,128)(2,1)} %get-tuple-element.26, bf16[1024,2048]{1,0:T(8,128)(2,1)} %param.16), kind=kOutput, calls=%fused_computation.65 | convolution fusion | flops 3228696576 | bytes 9961472 | tf_op jit(solution)/shard_map/dot_general | solution.py:338
  131.1 0.5 collective-permute-start.5
  131.6 13.3 %collective-permute-done.1.refs_1_ = bf16[384,512]{1,0:T(8,128)(2,1)} collective-permute-done((bf16[384,512]{1,0:T(8,128)(2,1)S(1)}, bf16[384,512]{1,0:T(8,128)(2,1)}, u32[]{:S(2)}, u32[]{:S(2)}) %collective-permute-start.1) | collective-permute-done | bytes 393248 | tf_op jit(solution)/shard_map/ppermute | solution.py:295
  144.9 3.3 %joined.4 = (bf16[384,1024]{1,0:T(8,128)(2,1)}, bf16[384,1024]{1,0:T(8,128)(2,1)}) custom-call(s32[1]{0:T(128)} %bitcast.2.me_ref, f32[1,1024]{1,0:T(1,128)} %bitcast.70, bf16[384,512]{1,0:T(8,128)(2,1)} %bitcast.62, bf16[384,512]{1,0:T(8,128)(2,1)} %collective-permute-done.1.refs_1_), custom_call_target="tpu_custom_call" | custom-call | flops 2359296 | bytes 2359296 | tf_op jit(solution)/shard_map/joined/pallas_call | solution.py:251
  148.2 8.2 %fusion.56.refs_1_ = bf16[384,1024]{1,0:T(8,128)(2,1)} fusion(bf16[2048,1024]{1,0:T(8,128)(2,1)} %param.17, bf16[384,1024]{1,0:T(8,128)(2,1)} %get-tuple-element.22, bf16[1024,2048]{1,0:T(8,128)(2,1)} %param.16), kind=kOutput, calls=%fused_computation.64 | convolution fusion | flops 3228696576 | bytes 9961472 | tf_op jit(solution)/shard_map/dot_general | solution.py:338
  156.9 0.9 copy-done.2
  157.8 3.6 %encoded_rows.7 = bf16[384,1024]{1,0:T(8,128)(2,1)} custom-call(f32[1,1024]{1,0:T(1,128)} %bitcast.71, bf16[384,1024]{1,0:T(8,128)(2,1)} %get-tuple-element.31.refs_0_, bf16[384,1024]{1,0:T(8,128)(2,1)} %copy-done.1, bf16[384,1024]{1,0:T(8,128)(2,1)} %copy-done.2), custom_call_target="tpu_custom_call" | custom-call | flops 2359296 | bytes 3145728 | tf_op jit(solution)/shard_map/encoded_rows/pallas_call | solution.py:279
  161.4 5.5 %convolution_convert_fusion.2 = bf16[384,2048]{1,0:T(8,128)(2,1)} fusion(bf16[384,1024]{1,0:T(8,128)(2,1)} %encoded_rows.7, bf16[1024,2048]{1,0:T(8,128)(2,1)} %param.18), kind=kOutput, calls=%fused_computation.38 | convolution fusion | flops 1611399168 | bytes 6553600 | tf_op jit(solution)/shard_map/dot_general | solution.py:346
  167.0 3.0 %convolution_convert_fusion = bf16[384,2048]{1,0:T(8,128)(2,1)} fusion(bf16[384,1024]{1,0:T(8,128)(2,1)S(1)} %copy-done.5, bf16[1024,2048]{1,0:T(8,128)(2,1)S(1)} %copy-done.12), kind=kOutput, calls=%fused_computation.36 | convolution fusion | flops 1611399168 | bytes 6553600 | tf_op jit(solution)/shard_map/dot_general | solution.py:347
  169.9 0.9 copy-done.4
  170.8 3.6 %encoded_rows.6 = bf16[384,1024]{1,0:T(8,128)(2,1)} custom-call(f32[1,1024]{1,0:T(1,128)} %bitcast.72, bf16[384,1024]{1,0:T(8,128)(2,1)} %get-tuple-element.28.refs_0_, bf16[384,1024]{1,0:T(8,128)(2,1)} %copy-done.3, bf16[384,1024]{1,0:T(8,128)(2,1)} %copy-done.4), custom_call_target="tpu_custom_call" | custom-call | flops 2359296 | bytes 3145728 | tf_op jit(solution)/shard_map/encoded_rows/pallas_call | solution.py:279
  174.4 5.5 %convolution_convert_fusion.3 = bf16[384,2048]{1,0:T(8,128)(2,1)} fusion(bf16[384,1024]{1,0:T(8,128)(2,1)} %encoded_rows.6, bf16[1024,2048]{1,0:T(8,128)(2,1)} %param.18), kind=kOutput, calls=%fused_computation.39 | convolution fusion | flops 1611399168 | bytes 6553600 | tf_op jit(solution)/shard_map/dot_general | solution.py:346
  179.9 3.0 %convolution_convert_fusion.1 = bf16[384,2048]{1,0:T(8,128)(2,1)} fusion(bf16[384,1024]{1,0:T(8,128)(2,1)S(1)} %copy-done.6, bf16[1024,2048]{1,0:T(8,128)(2,1)S(1)} %copy-done.13), kind=kOutput, calls=%fused_computation.37 | convolution fusion | flops 1611399168 | bytes 6553600 | tf_op jit(solution)/shard_map/dot_general | solution.py:347
  182.9 6.7 %attend.2.refs_4_ = bf16[3,128,2048]{2,1,0:T(8,128)(2,1)} custom-call(s32[1]{0:T(128)} %constant.19.clone.1.has_ref, bf16[3,128,2048]{2,1,0:T(8,128)(2,1)} %query_ref.3, bf16[3,2,64,2048]{3,2,1,0:T(8,128)(2,1)} %bitcast.57, bf16[3,2,64,2048]{3,2,1,0:T(8,128)(2,1)} %bitcast.53, bf16[3,2,64,2048]{3,2,1,0:T(8,128)(2,1)} %bitcast.58, ...), custom_call_target="tpu_custom_call" | custom-call | flops 402653184 | bytes 6291456 | tf_op jit(solution)/shard_map/attend/pallas_call | solution.py:212
  189.6 3.6 %encoded_rows.5 = bf16[384,1024]{1,0:T(8,128)(2,1)} custom-call(f32[1,1024]{1,0:T(1,128)} %bitcast.73, bf16[384,1024]{1,0:T(8,128)(2,1)} %get-tuple-element.25.refs_0_, bf16[384,1024]{1,0:T(8,128)(2,1)} %fusion.59.refs_1_, bf16[384,1024]{1,0:T(8,128)(2,1)} %collective-permute-done.5.refs_2_), custom_call_target="tpu_custom_call" | custom-call | flops 2359296 | bytes 3145728 | tf_op jit(solution)/shard_map/encoded_rows/pallas_call | solution.py:279
  193.2 5.5 %convolution_convert_fusion.6 = bf16[384,2048]{1,0:T(8,128)(2,1)} fusion(bf16[384,1024]{1,0:T(8,128)(2,1)} %encoded_rows.5, bf16[1024,2048]{1,0:T(8,128)(2,1)} %param.18), kind=kOutput, calls=%fused_computation.42 | convolution fusion | flops 1611399168 | bytes 6553600 | tf_op jit(solution)/shard_map/dot_general | solution.py:346
  198.8 3.0 %convolution_convert_fusion.4 = bf16[384,2048]{1,0:T(8,128)(2,1)} fusion(bf16[384,1024]{1,0:T(8,128)(2,1)S(1)} %copy-done.7, bf16[1024,2048]{1,0:T(8,128)(2,1)S(1)} %copy-done.14), kind=kOutput, calls=%fused_computation.40 | convolution fusion | flops 1611399168 | bytes 6553600 | tf_op jit(solution)/shard_map/dot_general | solution.py:347
  201.8 3.6 %encoded_rows.4 = bf16[384,1024]{1,0:T(8,128)(2,1)} custom-call(f32[1,1024]{1,0:T(1,128)} %bitcast.74, bf16[384,1024]{1,0:T(8,128)(2,1)} %get-tuple-element.21.refs_0_, bf16[384,1024]{1,0:T(8,128)(2,1)} %fusion.56.refs_1_, bf16[384,1024]{1,0:T(8,128)(2,1)} %collective-permute-done.2.refs_2_), custom_call_target="tpu_custom_call" | custom-call | flops 2359296 | bytes 3145728 | tf_op jit(solution)/shard_map/encoded_rows/pallas_call | solution.py:279
  205.3 5.5 %convolution_convert_fusion.5 = bf16[384,2048]{1,0:T(8,128)(2,1)} fusion(bf16[384,1024]{1,0:T(8,128)(2,1)} %encoded_rows.4, bf16[1024,2048]{1,0:T(8,128)(2,1)} %param.19), kind=kOutput, calls=%fused_computation.41 | convolution fusion | flops 1611399168 | bytes 6553600 | tf_op jit(solution)/shard_map/dot_general | solution.py:347
  210.9 3.0 %convolution_convert_fusion.7 = bf16[384,2048]{1,0:T(8,128)(2,1)} fusion(bf16[384,1024]{1,0:T(8,128)(2,1)S(1)} %copy-done.8, bf16[1024,2048]{1,0:T(8,128)(2,1)S(1)} %copy-done.15), kind=kOutput, calls=%fused_computation.43 | convolution fusion | flops 1611399168 | bytes 6553600 | tf_op jit(solution)/shard_map/dot_general | solution.py:346
  213.9 6.7 %attend.3 = bf16[3,128,2048]{2,1,0:T(8,128)(2,1)} custom-call(s32[1]{0:T(128)} %bitcast.has_ref, bf16[3,128,2048]{2,1,0:T(8,128)(2,1)} %query_ref.3, bf16[3,2,64,2048]{3,2,1,0:T(8,128)(2,1)} %bitcast.56, bf16[3,2,64,2048]{3,2,1,0:T(8,128)(2,1)} %bitcast.51, bf16[3,2,64,2048]{3,2,1,0:T(8,128)(2,1)} %bitcast.55, ...), custom_call_target="tpu_custom_call", output_to_operand_aliasing={{}: (6, {})} | custom-call | flops 402653184 | bytes 6291456 | tf_op jit(solution)/shard_map/attend/pallas_call | solution.py:212
  (36 shorter events, 0.6 us)
Async XLA Ops:
  39.6 29.2 %all-to-all-start = ((bf16[8,2,64,512]{3,2,1,0:T(8,128)(2,1)}), bf16[8,2,64,512]{3,2,1,0:T(8,128)(2,1)S(1)}, u32[]{:S(2)}, u32[]{:S(2)}) async-start(bf16[8,2,64,512]{3,2,1,0:T(8,128)(2,1)} %bitcast.59), calls=%async_computation | async-start | bytes 2097152 | tf_op jit(solution)/shard_map/all_to_all | solution.py:319
  46.0 33.4 %collective-permute-start.8 = (bf16[384,512]{1,0:T(8,128)(2,1)}, bf16[384,512]{1,0:T(8,128)(2,1)S(1)}, u32[]{:S(2)}, u32[]{:S(2)}) collective-permute-start(bf16[384,512]{1,0:T(8,128)(2,1)} %bitcast.63), channel_id=1, source_target_pairs={{0,1},{1,0},{2,3},{3,2},{4,5},{5,4},{6,7},{7,6},{8,9},{9,8},{10,11... | collective-permute-start | bytes 1179656 | tf_op jit(solution)/shard_map/ppermute | solution.py:295
  68.8 1.0 copy-start
  72.5 20.2 %collective-permute-start.6 = (bf16[384,512]{1,0:T(8,128)(2,1)}, bf16[384,512]{1,0:T(8,128)(2,1)S(1)}, u32[]{:S(2)}, u32[]{:S(2)}) collective-permute-start(bf16[384,512]{1,0:T(8,128)(2,1)} %bitcast.65), channel_id=1, source_target_pairs={{0,1},{1,0},{2,3},{3,2},{4,5},{5,4},{6,7},{7,6},{8,9},{9,8},{10,11... | collective-permute-start | bytes 1179656 | tf_op jit(solution)/shard_map/ppermute | solution.py:295
  74.1 17.1 %collective-permute-start.3 = (bf16[6,64,512]{2,1,0:T(8,128)(2,1)}, bf16[6,64,512]{2,1,0:T(8,128)(2,1)}, u32[]{:S(2)}, u32[]{:S(2)}) collective-permute-start(bf16[6,64,512]{2,1,0:T(8,128)(2,1)} %get-tuple-element.24), channel_id=1, source_target_pairs={{0,2},{2,4},{4,6},{6,8},{8,10},{10,12},{12,14},{1,3},{3,5},{5,7},{... | collective-permute-start | bytes 1179656 | tf_op jit(solution)/shard_map/ppermute | solution.py:301
  78.0 26.7 %collective-permute-start = (bf16[6,64,512]{2,1,0:T(8,128)(2,1)}, bf16[6,64,512]{2,1,0:T(8,128)(2,1)S(1)}, u32[]{:S(2)}, u32[]{:S(2)}) collective-permute-start(bf16[6,64,512]{2,1,0:T(8,128)(2,1)} %get-tuple-element.20), channel_id=1, source_target_pairs={{0,2},{2,4},{4,6},{6,8},{8,10},{10,12},{12,14},{1,3},{3,5},{5,7},{... | collective-permute-start | bytes 1179656 | tf_op jit(solution)/shard_map/ppermute | solution.py:301
  79.3 0.8 copy-start.10
  90.6 13.4 %copy-start.1 = (bf16[384,1024]{1,0:T(8,128)(2,1)}, bf16[384,1024]{1,0:T(8,128)(2,1)S(1)}, u32[]{:S(2)}) copy-start(bf16[384,1024]{1,0:T(8,128)(2,1)S(1)} %fusion.65.refs_1_) | copy-start | bytes 2359300
  90.7 66.3 %collective-permute-start.9 = (bf16[384,1024]{1,0:T(8,128)(2,1)S(1)}, bf16[384,1024]{1,0:T(8,128)(2,1)S(1)}, u32[]{:S(2)}, u32[]{:S(2)}) collective-permute-start(bf16[384,1024]{1,0:T(8,128)(2,1)S(1)} %fusion.65.refs_1_), channel_id=1, source_target_pairs={{0,1},{1,0},{2,3},{3,2},{4,5},{5,4},{6,7},{7,6},{8,9},{9,8},{10,11... | collective-permute-start | bytes 2359304 | tf_op jit(solution)/shard_map/ppermute | solution.py:295
  91.2 28.4 %collective-permute-start.4 = (bf16[384,512]{1,0:T(8,128)(2,1)}, bf16[384,512]{1,0:T(8,128)(2,1)}, u32[]{:S(2)}, u32[]{:S(2)}) collective-permute-start(bf16[384,512]{1,0:T(8,128)(2,1)} %bitcast.11.refs_0_), channel_id=1, source_target_pairs={{0,1},{1,0},{2,3},{3,2},{4,5},{5,4},{6,7},{7,6},{8,9},{9,8},{10,11... | collective-permute-start | bytes 1179656 | tf_op jit(solution)/shard_map/ppermute | solution.py:295
  92.8 0.8 copy-start.11
  104.1 27.0 %copy-start.3 = (bf16[384,1024]{1,0:T(8,128)(2,1)}, bf16[384,1024]{1,0:T(8,128)(2,1)S(1)}, u32[]{:S(2)}) copy-start(bf16[384,1024]{1,0:T(8,128)(2,1)S(1)} %fusion.62.refs_1_) | copy-start | bytes 2359300
  104.1 65.8 %collective-permute-start.7 = (bf16[384,1024]{1,0:T(8,128)(2,1)S(1)}, bf16[384,1024]{1,0:T(8,128)(2,1)S(1)}, u32[]{:S(2)}, u32[]{:S(2)}) collective-permute-start(bf16[384,1024]{1,0:T(8,128)(2,1)S(1)} %fusion.62.refs_1_), channel_id=1, source_target_pairs={{0,1},{1,0},{2,3},{3,2},{4,5},{5,4},{6,7},{7,6},{8,9},{9,8},{10,11... | collective-permute-start | bytes 2359304 | tf_op jit(solution)/shard_map/ppermute | solution.py:295
  104.7 26.5 %copy-start.9 = (bf16[6,64,512]{2,1,0:T(8,128)(2,1)}, bf16[6,64,512]{2,1,0:T(8,128)(2,1)S(1)}, u32[]{:S(2)}) copy-start(bf16[6,64,512]{2,1,0:T(8,128)(2,1)S(1)} %collective-permute-done) | copy-start | bytes 1179652
  104.7 40.3 %collective-permute-start.1 = (bf16[384,512]{1,0:T(8,128)(2,1)S(1)}, bf16[384,512]{1,0:T(8,128)(2,1)}, u32[]{:S(2)}, u32[]{:S(2)}) collective-permute-start(bf16[384,512]{1,0:T(8,128)(2,1)S(1)} %bitcast.61), channel_id=1, source_target_pairs={{0,1},{1,0},{2,3},{3,2},{4,5},{5,4},{6,7},{7,6},{8,9},{9,8},{10,11... | collective-permute-start | bytes 1179656 | tf_op jit(solution)/shard_map/ppermute | solution.py:295
  131.1 58.5 %collective-permute-start.5 = (bf16[384,1024]{1,0:T(8,128)(2,1)}, bf16[384,1024]{1,0:T(8,128)(2,1)}, u32[]{:S(2)}, u32[]{:S(2)}) collective-permute-start(bf16[384,1024]{1,0:T(8,128)(2,1)} %fusion.59.refs_1_), channel_id=1, source_target_pairs={{0,1},{1,0},{2,3},{3,2},{4,5},{5,4},{6,7},{7,6},{8,9},{9,8},{10,11... | collective-permute-start | bytes 2359304 | tf_op jit(solution)/shard_map/ppermute | solution.py:295
  156.4 45.3 %collective-permute-start.2 = (bf16[384,1024]{1,0:T(8,128)(2,1)}, bf16[384,1024]{1,0:T(8,128)(2,1)}, u32[]{:S(2)}, u32[]{:S(2)}) collective-permute-start(bf16[384,1024]{1,0:T(8,128)(2,1)} %fusion.56.refs_1_), channel_id=1, source_target_pairs={{0,1},{1,0},{2,3},{3,2},{4,5},{5,4},{6,7},{7,6},{8,9},{9,8},{10,11... | collective-permute-start | bytes 2359304 | tf_op jit(solution)/shard_map/ppermute | solution.py:295
  156.9 0.9 copy-start.2
  161.4 5.6 %copy-start.5 = (bf16[384,1024]{1,0:T(8,128)(2,1)S(1)}, bf16[384,1024]{1,0:T(8,128)(2,1)}, u32[]{:S(2)}) copy-start(bf16[384,1024]{1,0:T(8,128)(2,1)} %encoded_rows.7) | copy-start | bytes 2359300
  161.4 5.6 %copy-start.12 = (bf16[1024,2048]{1,0:T(8,128)(2,1)S(1)}, bf16[1024,2048]{1,0:T(8,128)(2,1)}, u32[]{:S(2)}) copy-start(bf16[1024,2048]{1,0:T(8,128)(2,1)} %param.19) | copy-start | bytes 12582916
  169.9 0.9 copy-start.4
  174.4 5.5 %copy-start.6 = (bf16[384,1024]{1,0:T(8,128)(2,1)S(1)}, bf16[384,1024]{1,0:T(8,128)(2,1)}, u32[]{:S(2)}) copy-start(bf16[384,1024]{1,0:T(8,128)(2,1)} %encoded_rows.6) | copy-start | bytes 2359300
  174.4 5.5 %copy-start.13 = (bf16[1024,2048]{1,0:T(8,128)(2,1)S(1)}, bf16[1024,2048]{1,0:T(8,128)(2,1)}, u32[]{:S(2)}) copy-start(bf16[1024,2048]{1,0:T(8,128)(2,1)} %param.19) | copy-start | bytes 12582916
  193.2 5.6 %copy-start.7 = (bf16[384,1024]{1,0:T(8,128)(2,1)S(1)}, bf16[384,1024]{1,0:T(8,128)(2,1)}, u32[]{:S(2)}) copy-start(bf16[384,1024]{1,0:T(8,128)(2,1)} %encoded_rows.5) | copy-start | bytes 2359300
  193.2 5.6 %copy-start.14 = (bf16[1024,2048]{1,0:T(8,128)(2,1)S(1)}, bf16[1024,2048]{1,0:T(8,128)(2,1)}, u32[]{:S(2)}) copy-start(bf16[1024,2048]{1,0:T(8,128)(2,1)} %param.19) | copy-start | bytes 12582916
  205.3 5.5 %copy-start.8 = (bf16[384,1024]{1,0:T(8,128)(2,1)S(1)}, bf16[384,1024]{1,0:T(8,128)(2,1)}, u32[]{:S(2)}) copy-start(bf16[384,1024]{1,0:T(8,128)(2,1)} %encoded_rows.4) | copy-start | bytes 2359300
  205.3 5.5 %copy-start.15 = (bf16[1024,2048]{1,0:T(8,128)(2,1)S(1)}, bf16[1024,2048]{1,0:T(8,128)(2,1)}, u32[]{:S(2)}) copy-start(bf16[1024,2048]{1,0:T(8,128)(2,1)} %param.18) | copy-start | bytes 12582916
where the time goes:
time: 222 us; the launch traced here: 221 us
  matrix products  65.1 us (29%)
  Pallas kernels  49.7 us (22%)
  waiting for transfers between devices  48 us (22%)
  blocking collectives  33.2 us (15%)
  starting transfers between devices  17.2 us (8%)
  local copies, waits for them, and re-layouts  7.26 us (3%)
    all_to_all x1, blocking collectives, step(): lax.all_to_all(piece.reshape((shards, MOST) + piece.shape[1:]), 'seq', sp...  33.2 us
    dot_general x4, matrix products, encode(): jnp.dot(hidden, w_out, preferred_element_type=jnp.float32)  30.9 us
    ppermute x8, waiting for transfers between devices, swapped(): lax.ppermute(array, axis, [(i, (i + by) % peers) for i in range(peers)])  26.8 us
    all_to_all x1, waiting for transfers between devices, step(): lax.all_to_all(piece.reshape((shards, MOST) + piece.shape[1:]), 'seq', sp...  21.2 us
    dot_general x4, matrix products, encode(): jnp.dot(encoded, w_key, preferred_element_type=jnp.float32)  19.7 us
    dot_general x4, matrix products, encode(): jnp.dot(encoded, w_value, preferred_element_type=jnp.float32)  14.5 us
    pallas_call x4, Pallas kernels, encoded_rows(): pl.pallas_call(norm_kernel, grid=(rows // tile,), out_shape=jax.ShapeDtyp...  14.3 us
    pallas_call x2, Pallas kernels, attend(): pl.pallas_call(attend_kernel, grid=(sequences,), out_shape=jax.ShapeDtype...  13.4 us
  transfers between devices with their start and end apart: 11, of which 3 were waited for; matrix products, arithmetic and copies ran while one was open for 26% of the time, Pallas kernels for 16%

commit v1 on v0

--- a/solution.py
+++ b/solution.py
@@ -266,28 +266,44 @@
     )(me, gain.reshape(1, -1), *held)
 
 
-def norm_kernel(gain_ref, *refs):
-    total = refs[0][...].astype(jnp.float32)
-    for ref in refs[1:-1]:
-        total = total + ref[...].astype(jnp.float32)
-    refs[-1][...] = rms_scale(total, gain_ref[...]).astype(refs[-1].dtype)
-
-
-def encoded_rows(terms, gain, tile):
+def project_kernel(gain_ref, w_key_ref, w_value_ref, *refs):
+    term_refs, (key_ref, value_ref, encoded_ref) = refs[:-3], refs[-3:]
+
+    @pl.when(pl.program_id(0) == 0)
+    def _():
+        total = term_refs[0][...].astype(jnp.float32)
+        for ref in term_refs[1:]:
+            total = total + ref[...].astype(jnp.float32)
+        encoded_ref[...] = rms_scale(total, gain_ref[...]).astype(encoded_ref.dtype)
+
+    for weight_ref, out_ref in ((w_key_ref, key_ref), (w_value_ref, value_ref)):
+        out_ref[...] = jnp.dot(
+            encoded_ref[...], weight_ref[...], preferred_element_type=jnp.float32
+        ).astype(out_ref.dtype)
+
+
+def projected(terms, gain, w_key, w_value):
     rows, width = terms[0].shape
-    spec = pl.BlockSpec((tile, width), lambda i: (i, 0))
-    return pl.pallas_call(
-        norm_kernel,
-        grid=(rows // tile,),
-        out_shape=jax.ShapeDtypeStruct((rows, width), jnp.bfloat16),
-        in_specs=[pl.BlockSpec((1, width), lambda i: (0, 0))] + [spec] * len(terms),
-        out_specs=spec,
+    columns = w_key.shape[1]
+    tile = 512 if columns % 512 == 0 else columns
+    term_spec = pl.BlockSpec((rows, width), lambda i: (0, 0))
+    weight_spec = pl.BlockSpec((width, tile), lambda i: (0, i))
+    out_spec = pl.BlockSpec((rows, tile), lambda i: (0, i))
+    out = jax.ShapeDtypeStruct((rows, columns), jnp.bfloat16)
+    return pl.pallas_call(
+        project_kernel,
+        grid=(columns // tile,),
+        out_shape=[out, out],
+        in_specs=[pl.BlockSpec((1, width), lambda i: (0, 0)), weight_spec, weight_spec]
+        + [term_spec] * len(terms),
+        out_specs=[out_spec, out_spec],
+        scratch_shapes=[pltpu.VMEM((rows, width), jnp.bfloat16)],
         cost_estimate=pl.CostEstimate(
-            flops=6 * rows * width, bytes_accessed=2 * rows * width * (len(terms) + 1),
+            flops=4 * rows * width * columns, bytes_accessed=4 * (width + rows) * columns,
             transcendentals=rows,
         ),
-        name="encoded_rows",
-    )(gain.reshape(1, -1), *terms)
+        name="projected",
+    )(gain.reshape(1, -1), w_key, w_value, *terms)
 
 
 def swapped(array, axis, by):
@@ -339,14 +355,8 @@
             jnp.bfloat16
         )
         others = [swapped(partial, "mp", by) for by in range(1, peers)]
-        encoded = encoded_rows(
-            [blocks, partial, *others], out_gain, neigh * rows
-        )
+        keys, values = projected([blocks, partial, *others], out_gain, w_key, w_value)
         shape = (-1, neigh, rows, local_width)
-        keys = jnp.dot(encoded, w_key, preferred_element_type=jnp.float32).astype(jnp.bfloat16)
-        values = jnp.dot(encoded, w_value, preferred_element_type=jnp.float32).astype(
-            jnp.bfloat16
-        )
         return keys.reshape(shape), values.reshape(shape)
 
     kept_rows = [encode(piece) for piece in kept]

time: 222 us -> 206 us (0.928)
  matrix products: 65.1 us -> 30 us
  Pallas kernels: 49.7 us -> 69.2 us
    dot_general x8 -> x0, matrix products: 34.2 us -> none  [the longest x4 19.7 us: encode(): jnp.dot(encoded, w_key, preferred_element_type=jnp.float32)]
    pallas_call x4, Pallas kernels: 14.3 us -> 33.7 us  [projected(): pl.pallas_call(project_kernel, grid=(columns // tile,), out_shape=[out, o...]
    unnamed x34 -> x24, local copies, waits for them, and re-layouts: 5.89 us -> 6.53 us
  transfers between devices with their start and end apart: 11 -> 11, of which waited for: 3 -> 3; matrix products, arithmetic and copies ran while one was open for 26% -> 15% of each run, Pallas kernels for 16% -> 25%
where the time goes in v1:
time: 206 us; the launch traced here: 205 us
  Pallas kernels  69.2 us (34%)
  waiting for transfers between devices  47.2 us (23%)
  blocking collectives  33.2 us (16%)
  matrix products  30 us (15%)
  starting transfers between devices  17.1 us (8%)
  local copies, waits for them, and re-layouts  7.86 us (4%)
    pallas_call x4, Pallas kernels, projected(): pl.pallas_call(project_kernel, grid=(columns // tile,), out_shape=[out, o...  33.7 us
    all_to_all x1, blocking collectives, step(): lax.all_to_all(piece.reshape((shards, MOST) + piece.shape[1:]), 'seq', sp...  33.2 us
    dot_general x4, matrix products, encode(): jnp.dot(hidden, w_out, preferred_element_type=jnp.float32)  30 us
    ppermute x8, waiting for transfers between devices, swapped(): lax.ppermute(array, axis, [(i, (i + by) % peers) for i in range(peers)])  25.9 us
    all_to_all x1, waiting for transfers between devices, step(): lax.all_to_all(piece.reshape((shards, MOST) + piece.shape[1:]), 'seq', sp...  21.2 us
    pallas_call x2, Pallas kernels, attend(): pl.pallas_call(attend_kernel, grid=(sequences,), out_shape=jax.ShapeDtype...  13.4 us
    pallas_call x4, Pallas kernels, joined(): pl.pallas_call(join_kernel, grid=(rows // tile,), out_shape=[full, full],...  13.1 us
    ppermute x8, starting transfers between devices, swapped(): lax.ppermute(array, axis, [(i, (i + by) % peers) for i in range(peers)])  8.44 us
  transfers between devices with their start and end apart: 11, of which 3 were waited for; matrix products, arithmetic and copies ran while one was open for 15% of the time, Pallas kernels for 25%

profile of v1, /device:TPU:0, one launch (start us, length us, event | category | flops | bytes accessed | tf_op | source)
XLA Modules:
  0.0 204.7 jit_solution(10408436640751847954)
XLA Ops:
  0.0 0.8 copy.14
  0.8 0.6 reshape.86.owner_ref
  1.4 0.8 copy.15
  2.2 0.7 reshape.87.row_ref
  2.9 3.5 %gather_requests.1 = (bf16[16,64,512]{2,1,0:T(8,128)(2,1)}, bf16[16,64,512]{2,1,0:T(8,128)(2,1)}) custom-call(s32[1]{0:T(128)} %bitcast.4.my_ref, s32[96]{0:T(128)} %reshape.86.owner_ref, s32[96]{0:T(128)} %reshape.87.row_ref, bf16[32,128,512]{2,1,0:T(8,128)(2,1)} %database_ref.1), custom_call_target="tpu_custom_call" | custom-call | tf_op jit(solution)/shard_map/gather_requests/pallas_call | solution.py:77
  6.4 33.2 %all_to_all.10 = bf16[8,2,64,512]{3,2,1,0:T(8,128)(2,1)} all-to-all(bf16[8,2,64,512]{3,2,1,0:T(8,128)(2,1)} %bitcast.44), channel_id=1, replica_groups=mesh['dp'=2,'seq'=8,'mp'=2] {'seq'}, dimensions={0} | all-to-all | bytes 2097152 | tf_op jit(solution)/shard_map/all_to_all | solution.py:335
  39.6 3.6 %all-to-all-start = ((bf16[8,2,64,512]{3,2,1,0:T(8,128)(2,1)}), bf16[8,2,64,512]{3,2,1,0:T(8,128)(2,1)S(1)}, u32[]{:S(2)}, u32[]{:S(2)}) async-start(bf16[8,2,64,512]{3,2,1,0:T(8,128)(2,1)} %bitcast.43), calls=%async_computation | async-start | bytes 2097152 | tf_op jit(solution)/shard_map/all_to_all | solution.py:335
  43.2 2.7 %pick_blocks.3 = (bf16[6,64,512]{2,1,0:T(8,128)(2,1)}, bf16[6,64,512]{2,1,0:T(8,128)(2,1)}) custom-call(s32[1]{0:T(128)} %bitcast.4.my_ref, s32[96]{0:T(128)} %reshape.86.owner_ref, bf16[16,64,512]{2,1,0:T(8,128)(2,1)} %bitcast.34), custom_call_target="tpu_custom_call" | custom-call | tf_op jit(solution)/shard_map/pick_blocks/pallas_call | solution.py:137
  45.9 1.6 collective-permute-start.8
  47.5 21.2 %all-to-all-done = bf16[8,2,64,512]{3,2,1,0:T(8,128)(2,1)S(1)} async-done(((bf16[8,2,64,512]{3,2,1,0:T(8,128)(2,1)}), bf16[8,2,64,512]{3,2,1,0:T(8,128)(2,1)S(1)}, u32[]{:S(2)}, u32[]{:S(2)}) %all-to-all-start) | async-done | bytes 1048608 | tf_op jit(solution)/shard_map/all_to_all | solution.py:335
  68.8 1.0 copy-done
  69.7 2.8 %pick_blocks.2 = (bf16[6,64,512]{2,1,0:T(8,128)(2,1)}, bf16[6,64,512]{2,1,0:T(8,128)(2,1)}) custom-call(s32[1]{0:T(128)} %bitcast.4.my_ref, s32[96]{0:T(128)} %reshape.86.owner_ref, bf16[16,64,512]{2,1,0:T(8,128)(2,1)} %bitcast.33), custom_call_target="tpu_custom_call" | custom-call | tf_op jit(solution)/shard_map/pick_blocks/pallas_call | solution.py:137
  72.5 1.6 collective-permute-start.6
  74.1 3.2 %collective-permute-start.3 = (bf16[6,64,512]{2,1,0:T(8,128)(2,1)}, bf16[6,64,512]{2,1,0:T(8,128)(2,1)S(1)}, u32[]{:S(2)}, u32[]{:S(2)}) collective-permute-start(bf16[6,64,512]{2,1,0:T(8,128)(2,1)} %get-tuple-element.33), channel_id=1, source_target_pairs={{0,2},{2,4},{4,6},{6,8},{8,10},{10,12},{12,14},{1,3},{3,5},{5,7},{... | collective-permute-start | bytes 1179656 | tf_op jit(solution)/shard_map/ppermute | solution.py:317
  77.3 1.9 collective-permute-start
  79.2 0.0 collective-permute-done.8.refs_1_
  79.2 0.8 copy-done.3
  80.0 3.3 %joined.7 = (bf16[384,1024]{1,0:T(8,128)(2,1)}, bf16[384,1024]{1,0:T(8,128)(2,1)}) custom-call(s32[1]{0:T(128)} %bitcast.2.me_ref, f32[1,1024]{1,0:T(1,128)} %bitcast.53, bf16[384,512]{1,0:T(8,128)(2,1)} %bitcast.50, bf16[384,512]{1,0:T(8,128)(2,1)} %copy-done.3), custom_call_target="tpu_custom_call" | custom-call | flops 2359296 | bytes 2359296 | tf_op jit(solution)/shard_map/joined/pallas_call | solution.py:251
  83.2 7.3 %fusion.65.refs_1_ = bf16[384,1024]{1,0:T(8,128)(2,1)S(1)} fusion(bf16[2048,1024]{1,0:T(8,128)(2,1)} %param.17, bf16[384,1024]{1,0:T(8,128)(2,1)} %get-tuple-element.45, bf16[1024,2048]{1,0:T(8,128)(2,1)} %param.16), kind=kOutput, calls=%fused_computation.59 | convolution fusion | flops 3228696576 | bytes 9961472 | tf_op jit(solution)/shard_map/dot_general | solution.py:354
  90.5 0.6 collective-permute-start.9
  91.1 0.0 collective-permute-done.3
  91.1 1.5 collective-permute-start.4
  92.6 0.0 collective-permute-done.6.refs_1_
  92.6 0.8 copy-done.4
  93.4 3.3 %joined.6 = (bf16[384,1024]{1,0:T(8,128)(2,1)}, bf16[384,1024]{1,0:T(8,128)(2,1)}) custom-call(s32[1]{0:T(128)} %bitcast.2.me_ref, f32[1,1024]{1,0:T(1,128)} %bitcast.54, bf16[384,512]{1,0:T(8,128)(2,1)} %bitcast.52, bf16[384,512]{1,0:T(8,128)(2,1)} %copy-done.4), custom_call_target="tpu_custom_call" | custom-call | flops 2359296 | bytes 2359296 | tf_op jit(solution)/shard_map/joined/pallas_call | solution.py:251
  96.7 8.2 %fusion.62.refs_1_ = bf16[384,1024]{1,0:T(8,128)(2,1)} fusion(bf16[2048,1024]{1,0:T(8,128)(2,1)} %param.17, bf16[384,1024]{1,0:T(8,128)(2,1)} %get-tuple-element.41, bf16[1024,2048]{1,0:T(8,128)(2,1)} %param.16), kind=kOutput, calls=%fused_computation.58 | convolution fusion | flops 3228696576 | bytes 9961472 | tf_op jit(solution)/shard_map/dot_general | solution.py:354
  104.8 0.5 collective-permute-start.7
  105.4 0.0 collective-permute-done
  105.4 1.5 collective-permute-start.1
  106.9 12.6 %collective-permute-done.4.refs_1_ = bf16[384,512]{1,0:T(8,128)(2,1)S(1)} collective-permute-done((bf16[384,512]{1,0:T(8,128)(2,1)S(1)}, bf16[384,512]{1,0:T(8,128)(2,1)S(1)}, u32[]{:S(2)}, u32[]{:S(2)}) %collective-permute-start.4) | collective-permute-done | bytes 393248 | tf_op jit(solution)/shard_map/ppermute | solution.py:311
  119.4 0.8 copy-done.5
  120.2 3.3 %joined.5 = (bf16[384,1024]{1,0:T(8,128)(2,1)}, bf16[384,1024]{1,0:T(8,128)(2,1)}) custom-call(s32[1]{0:T(128)} %bitcast.2.me_ref, f32[1,1024]{1,0:T(1,128)} %bitcast.55, bf16[384,512]{1,0:T(8,128)(2,1)} %bitcast.48, bf16[384,512]{1,0:T(8,128)(2,1)} %copy-done.5), custom_call_target="tpu_custom_call" | custom-call | flops 2359296 | bytes 2359296 | tf_op jit(solution)/shard_map/joined/pallas_call | solution.py:251
  123.5 7.3 %fusion.59.refs_1_ = bf16[384,1024]{1,0:T(8,128)(2,1)S(1)} fusion(bf16[2048,1024]{1,0:T(8,128)(2,1)} %param.17, bf16[384,1024]{1,0:T(8,128)(2,1)} %get-tuple-element.35, bf16[1024,2048]{1,0:T(8,128)(2,1)} %param.16), kind=kOutput, calls=%fused_computation.57 | convolution fusion | flops 3228696576 | bytes 9961472 | tf_op jit(solution)/shard_map/dot_general | solution.py:354
  130.8 0.6 collective-permute-start.5
  131.3 13.4 %collective-permute-done.1.refs_1_ = bf16[384,512]{1,0:T(8,128)(2,1)S(1)} collective-permute-done((bf16[384,512]{1,0:T(8,128)(2,1)S(1)}, bf16[384,512]{1,0:T(8,128)(2,1)S(1)}, u32[]{:S(2)}, u32[]{:S(2)}) %collective-permute-start.1) | collective-permute-done | bytes 393248 | tf_op jit(solution)/shard_map/ppermute | solution.py:311
  144.7 0.8 copy-done.6
  145.5 3.3 %joined.4 = (bf16[384,1024]{1,0:T(8,128)(2,1)}, bf16[384,1024]{1,0:T(8,128)(2,1)}) custom-call(s32[1]{0:T(128)} %bitcast.2.me_ref, f32[1,1024]{1,0:T(1,128)} %bitcast.56, bf16[384,512]{1,0:T(8,128)(2,1)} %bitcast.46, bf16[384,512]{1,0:T(8,128)(2,1)} %copy-done.6), custom_call_target="tpu_custom_call" | custom-call | flops 2359296 | bytes 2359296 | tf_op jit(solution)/shard_map/joined/pallas_call | solution.py:251
  148.7 7.3 %fusion.56.refs_1_ = bf16[384,1024]{1,0:T(8,128)(2,1)S(1)} fusion(bf16[2048,1024]{1,0:T(8,128)(2,1)} %param.17, bf16[384,1024]{1,0:T(8,128)(2,1)} %get-tuple-element.30, bf16[1024,2048]{1,0:T(8,128)(2,1)} %param.16), kind=kOutput, calls=%fused_computation.56 | convolution fusion | flops 3228696576 | bytes 9961472 | tf_op jit(solution)/shard_map/dot_general | solution.py:354
  156.0 0.6 collective-permute-start.2
  156.6 0.0 collective-permute-done.9.refs_2_
  156.6 0.9 copy-done.8
  157.5 8.4 %projected.7 = (bf16[384,2048]{1,0:T(8,128)(2,1)}, bf16[384,2048]{1,0:T(8,128)(2,1)}) custom-call(f32[1,1024]{1,0:T(1,128)} %bitcast.57, bf16[1024,2048]{1,0:T(8,128)(2,1)} %w_key_ref.7, bf16[1024,2048]{1,0:T(8,128)(2,1)} %w_value_ref.7, bf16[384,1024]{1,0:T(8,128)(2,1)} %get-tuple-element.44.refs_0_, bf16[384,1024]{1,0:T(8,128)(2,1)} %copy-done.7, ...), custom_call_target="tpu_custom_call" | custom-call | flops 3221225472 | bytes 11534336 | tf_op jit(solution)/shard_map/projected/pallas_call | solution.py:293
  165.9 0.0 collective-permute-done.7.refs_2_
  165.9 8.4 %projected.6 = (bf16[384,2048]{1,0:T(8,128)(2,1)}, bf16[384,2048]{1,0:T(8,128)(2,1)}) custom-call(f32[1,1024]{1,0:T(1,128)} %bitcast.58, bf16[1024,2048]{1,0:T(8,128)(2,1)} %w_key_ref.7, bf16[1024,2048]{1,0:T(8,128)(2,1)} %w_value_ref.7, bf16[384,1024]{1,0:T(8,128)(2,1)} %get-tuple-element.40.refs_0_, bf16[384,1024]{1,0:T(8,128)(2,1)} %fusion.62.refs_1_, ...), custom_call_target="tpu_custom_call" | custom-call | flops 3221225472 | bytes 11534336 | tf_op jit(solution)/shard_map/projected/pallas_call | solution.py:293
  174.4 6.7 %attend.2.refs_4_ = bf16[3,128,2048]{2,1,0:T(8,128)(2,1)} custom-call(s32[1]{0:T(128)} %constant.19.clone.1.has_ref, bf16[3,128,2048]{2,1,0:T(8,128)(2,1)} %query_ref.3, bf16[3,2,64,2048]{3,2,1,0:T(8,128)(2,1)} %bitcast.41, bf16[3,2,64,2048]{3,2,1,0:T(8,128)(2,1)} %bitcast.37, bf16[3,2,64,2048]{3,2,1,0:T(8,128)(2,1)} %bitcast.42, ...), custom_call_target="tpu_custom_call" | custom-call | flops 402653184 | bytes 6291456 | tf_op jit(solution)/shard_map/attend/pallas_call | solution.py:212
  181.1 8.4 %projected.5 = (bf16[384,2048]{1,0:T(8,128)(2,1)}, bf16[384,2048]{1,0:T(8,128)(2,1)}) custom-call(f32[1,1024]{1,0:T(1,128)} %bitcast.59, bf16[1024,2048]{1,0:T(8,128)(2,1)} %w_key_ref.7, bf16[1024,2048]{1,0:T(8,128)(2,1)} %w_value_ref.7, bf16[384,1024]{1,0:T(8,128)(2,1)} %get-tuple-element.34.refs_0_, bf16[384,1024]{1,0:T(8,128)(2,1)} %copy-done.9, ...), custom_call_target="tpu_custom_call" | custom-call | flops 3221225472 | bytes 11534336 | tf_op jit(solution)/shard_map/projected/pallas_call | solution.py:293
  189.5 8.4 %projected.4 = (bf16[384,2048]{1,0:T(8,128)(2,1)}, bf16[384,2048]{1,0:T(8,128)(2,1)}) custom-call(f32[1,1024]{1,0:T(1,128)} %bitcast.60, bf16[1024,2048]{1,0:T(8,128)(2,1)} %w_key_ref.7, bf16[1024,2048]{1,0:T(8,128)(2,1)} %w_value_ref.7, bf16[384,1024]{1,0:T(8,128)(2,1)} %get-tuple-element.29.refs_0_, bf16[384,1024]{1,0:T(8,128)(2,1)} %copy-done.10, ...), custom_call_target="tpu_custom_call" | custom-call | flops 3221225472 | bytes 11534336 | tf_op jit(solution)/shard_map/projected/pallas_call | solution.py:293
  198.0 6.7 %attend.3 = bf16[3,128,2048]{2,1,0:T(8,128)(2,1)} custom-call(s32[1]{0:T(128)} %bitcast.has_ref, bf16[3,128,2048]{2,1,0:T(8,128)(2,1)} %query_ref.3, bf16[3,2,64,2048]{3,2,1,0:T(8,128)(2,1)} %bitcast.39, bf16[3,2,64,2048]{3,2,1,0:T(8,128)(2,1)} %bitcast.35, bf16[3,2,64,2048]{3,2,1,0:T(8,128)(2,1)} %bitcast.40, ...), custom_call_target="tpu_custom_call", output_to_operand_aliasing={{}: (6, {})} | custom-call | flops 402653184 | bytes 6291456 | tf_op jit(solution)/shard_map/attend/pallas_call | solution.py:212
  (18 shorter events, 0.0 us)
Async XLA Ops:
  39.6 29.2 %all-to-all-start = ((bf16[8,2,64,512]{3,2,1,0:T(8,128)(2,1)}), bf16[8,2,64,512]{3,2,1,0:T(8,128)(2,1)S(1)}, u32[]{:S(2)}, u32[]{:S(2)}) async-start(bf16[8,2,64,512]{3,2,1,0:T(8,128)(2,1)} %bitcast.43), calls=%async_computation | async-start | bytes 2097152 | tf_op jit(solution)/shard_map/all_to_all | solution.py:335
  45.9 33.3 %collective-permute-start.8 = (bf16[384,512]{1,0:T(8,128)(2,1)}, bf16[384,512]{1,0:T(8,128)(2,1)S(1)}, u32[]{:S(2)}, u32[]{:S(2)}) collective-permute-start(bf16[384,512]{1,0:T(8,128)(2,1)} %bitcast.49), channel_id=1, source_target_pairs={{0,1},{1,0},{2,3},{3,2},{4,5},{5,4},{6,7},{7,6},{8,9},{9,8},{10,11... | collective-permute-start | bytes 1179656 | tf_op jit(solution)/shard_map/ppermute | solution.py:311
  68.7 1.0 copy-start
  72.5 20.1 %collective-permute-start.6 = (bf16[384,512]{1,0:T(8,128)(2,1)}, bf16[384,512]{1,0:T(8,128)(2,1)S(1)}, u32[]{:S(2)}, u32[]{:S(2)}) collective-permute-start(bf16[384,512]{1,0:T(8,128)(2,1)} %bitcast.51), channel_id=1, source_target_pairs={{0,1},{1,0},{2,3},{3,2},{4,5},{5,4},{6,7},{7,6},{8,9},{9,8},{10,11... | collective-permute-start | bytes 1179656 | tf_op jit(solution)/shard_map/ppermute | solution.py:311
  74.1 17.0 %collective-permute-start.3 = (bf16[6,64,512]{2,1,0:T(8,128)(2,1)}, bf16[6,64,512]{2,1,0:T(8,128)(2,1)S(1)}, u32[]{:S(2)}, u32[]{:S(2)}) collective-permute-start(bf16[6,64,512]{2,1,0:T(8,128)(2,1)} %get-tuple-element.33), channel_id=1, source_target_pairs={{0,2},{2,4},{4,6},{6,8},{8,10},{10,12},{12,14},{1,3},{3,5},{5,7},{... | collective-permute-start | bytes 1179656 | tf_op jit(solution)/shard_map/ppermute | solution.py:317
  77.3 28.1 %collective-permute-start = (bf16[6,64,512]{2,1,0:T(8,128)(2,1)}, bf16[6,64,512]{2,1,0:T(8,128)(2,1)S(1)}, u32[]{:S(2)}, u32[]{:S(2)}) collective-permute-start(bf16[6,64,512]{2,1,0:T(8,128)(2,1)} %get-tuple-element.28), channel_id=1, source_target_pairs={{0,2},{2,4},{4,6},{6,8},{8,10},{10,12},{12,14},{1,3},{3,5},{5,7},{... | collective-permute-start | bytes 1179656 | tf_op jit(solution)/shard_map/ppermute | solution.py:317
  79.2 0.8 copy-start.3
  90.5 14.3 %copy-start.7 = (bf16[384,1024]{1,0:T(8,128)(2,1)}, bf16[384,1024]{1,0:T(8,128)(2,1)S(1)}, u32[]{:S(2)}) copy-start(bf16[384,1024]{1,0:T(8,128)(2,1)S(1)} %fusion.65.refs_1_) | copy-start | bytes 2359300
  90.5 66.1 %collective-permute-start.9 = (bf16[384,1024]{1,0:T(8,128)(2,1)S(1)}, bf16[384,1024]{1,0:T(8,128)(2,1)S(1)}, u32[]{:S(2)}, u32[]{:S(2)}) collective-permute-start(bf16[384,1024]{1,0:T(8,128)(2,1)S(1)} %fusion.65.refs_1_), channel_id=1, source_target_pairs={{0,1},{1,0},{2,3},{3,2},{4,5},{5,4},{6,7},{7,6},{8,9},{9,8},{10,11... | collective-permute-start | bytes 2359304 | tf_op jit(solution)/shard_map/ppermute | solution.py:311
  91.1 13.7 %copy-start.2 = (bf16[6,64,512]{2,1,0:T(8,128)(2,1)}, bf16[6,64,512]{2,1,0:T(8,128)(2,1)S(1)}, u32[]{:S(2)}) copy-start(bf16[6,64,512]{2,1,0:T(8,128)(2,1)S(1)} %collective-permute-done.3) | copy-start | bytes 1179652
  91.1 28.3 %collective-permute-start.4 = (bf16[384,512]{1,0:T(8,128)(2,1)S(1)}, bf16[384,512]{1,0:T(8,128)(2,1)S(1)}, u32[]{:S(2)}, u32[]{:S(2)}) collective-permute-start(bf16[384,512]{1,0:T(8,128)(2,1)S(1)} %bitcast.47), channel_id=1, source_target_pairs={{0,1},{1,0},{2,3},{3,2},{4,5},{5,4},{6,7},{7,6},{8,9},{9,8},{10,11... | collective-permute-start | bytes 1179656 | tf_op jit(solution)/shard_map/ppermute | solution.py:311
  92.6 0.8 copy-start.4
  104.8 61.1 %collective-permute-start.7 = (bf16[384,1024]{1,0:T(8,128)(2,1)}, bf16[384,1024]{1,0:T(8,128)(2,1)}, u32[]{:S(2)}, u32[]{:S(2)}) collective-permute-start(bf16[384,1024]{1,0:T(8,128)(2,1)} %fusion.62.refs_1_), channel_id=1, source_target_pairs={{0,1},{1,0},{2,3},{3,2},{4,5},{5,4},{6,7},{7,6},{8,9},{9,8},{10,11... | collective-permute-start | bytes 2359304 | tf_op jit(solution)/shard_map/ppermute | solution.py:311
  105.4 25.4 %copy-start.1 = (bf16[6,64,512]{2,1,0:T(8,128)(2,1)}, bf16[6,64,512]{2,1,0:T(8,128)(2,1)S(1)}, u32[]{:S(2)}) copy-start(bf16[6,64,512]{2,1,0:T(8,128)(2,1)S(1)} %collective-permute-done) | copy-start | bytes 1179652
  105.4 39.4 %collective-permute-start.1 = (bf16[384,512]{1,0:T(8,128)(2,1)S(1)}, bf16[384,512]{1,0:T(8,128)(2,1)S(1)}, u32[]{:S(2)}, u32[]{:S(2)}) collective-permute-start(bf16[384,512]{1,0:T(8,128)(2,1)S(1)} %bitcast.45), channel_id=1, source_target_pairs={{0,1},{1,0},{2,3},{3,2},{4,5},{5,4},{6,7},{7,6},{8,9},{9,8},{10,11... | collective-permute-start | bytes 1179656 | tf_op jit(solution)/shard_map/ppermute | solution.py:311
  119.4 0.8 copy-start.5
  130.8 25.3 %copy-start.9 = (bf16[384,1024]{1,0:T(8,128)(2,1)}, bf16[384,1024]{1,0:T(8,128)(2,1)S(1)}, u32[]{:S(2)}) copy-start(bf16[384,1024]{1,0:T(8,128)(2,1)S(1)} %fusion.59.refs_1_) | copy-start | bytes 2359300
  130.8 50.3 %collective-permute-start.5 = (bf16[384,1024]{1,0:T(8,128)(2,1)S(1)}, bf16[384,1024]{1,0:T(8,128)(2,1)}, u32[]{:S(2)}, u32[]{:S(2)}) collective-permute-start(bf16[384,1024]{1,0:T(8,128)(2,1)S(1)} %fusion.59.refs_1_), channel_id=1, source_target_pairs={{0,1},{1,0},{2,3},{3,2},{4,5},{5,4},{6,7},{7,6},{8,9},{9,8},{10,11... | collective-permute-start | bytes 2359304 | tf_op jit(solution)/shard_map/ppermute | solution.py:311
  144.7 0.8 copy-start.6
  156.0 18.3 %copy-start.10 = (bf16[384,1024]{1,0:T(8,128)(2,1)}, bf16[384,1024]{1,0:T(8,128)(2,1)S(1)}, u32[]{:S(2)}) copy-start(bf16[384,1024]{1,0:T(8,128)(2,1)S(1)} %fusion.56.refs_1_) | copy-start | bytes 2359300
  156.0 33.5 %collective-permute-start.2 = (bf16[384,1024]{1,0:T(8,128)(2,1)S(1)}, bf16[384,1024]{1,0:T(8,128)(2,1)}, u32[]{:S(2)}, u32[]{:S(2)}) collective-permute-start(bf16[384,1024]{1,0:T(8,128)(2,1)S(1)} %fusion.56.refs_1_), channel_id=1, source_target_pairs={{0,1},{1,0},{2,3},{3,2},{4,5},{5,4},{6,7},{7,6},{8,9},{9,8},{10,11... | collective-permute-start | bytes 2359304 | tf_op jit(solution)/shard_map/ppermute | solution.py:311
  156.6 0.9 copy-start.8
